TPU v7x, 768 devices: a whole 4x8x12 slice. The times are simulated.
768 devices in a mesh: grp: 8 (over x, core), rep: 96 (over z, y).
Axes of the slice: x: 4, y: 8, z: 12, core: 2. Of those that a mesh axis runs over, the one named last changes fastest.
Arguments:
- blocks: bfloat16 [1536, 64, 4096], P(('grp', 'rep')), may hold values from 0 to 10
- coords: int32 [1536, 3], P(('grp', 'rep')), may hold values from 0 to 767, as said below
- factor_a: float32 [49152, 128], P(('grp', 'rep')), may hold values from 0 to 1
- factor_b: bfloat16 [8192, 128], P('grp'), may hold values from 0.049804688 to 1
- factor_c: bfloat16 [8192, 128], P('grp'), may hold values from 0.049804688 to 1
Outputs:
- updated_a: float32 [49152, 128], P(('grp', 'rep'))
Inputs may be any that keep to these rules, and one draw needn't show every extreme that they name: Row n of coords holds first, second and third coordinates below 768, 128, 128. Among the 2 blocks of one device, for each mode, the values coordinate // 96 (first mode) or coordinate // 16 (second and third) take any one value at most 2 times.
All inputs are finite; a program needn't handle non-finite values.
Results may differ from a plain program's by a relative error of at most 0.00072.
Values may be sent and summed in bfloat16 or wider, within the bound.
A program may use at most 32 MiB of HBM per device.

v0:
```python
import jax
import jax.numpy as jnp
from jax import lax
from jax.sharding import PartitionSpec as P

R = 128
BS = 64
CAP = 2


def slot_of(owner):
    count = owner.shape[0]
    same_peer = owner[:, None] == owner[None, :]
    earlier = jnp.arange(count)[None, :] < jnp.arange(count)[:, None]
    return jnp.sum(jnp.logical_and(same_peer, earlier), axis=1)


def gram_of(factor):
    dims = (((0,), (0,)), ((), ()))
    return lax.dot_general(factor, factor, dims, preferred_element_type=jnp.float32)


def body(blocks, coords, factor_a, factor_b, factor_c):
    n_grp = lax.axis_size("grp")
    n_rep = lax.axis_size("rep")
    nblk_here = blocks.shape[0]
    jb_here = factor_b.shape[0] // BS
    ab_here = factor_a.shape[0] // BS
    part_here = ab_here * n_rep
    first_row = coords[:, 0]
    second_row = coords[:, 1]
    third_row = coords[:, 2]
    peer_b = second_row // jb_here
    peer_c = third_row // jb_here
    slot_b = slot_of(peer_b)
    slot_c = slot_of(peer_c) + CAP
    wanted = jnp.zeros((n_grp, 2 * CAP), jnp.int32)
    wanted = wanted.at[peer_b, slot_b].set(second_row % jb_here)
    wanted = wanted.at[peer_c, slot_c].set(third_row % jb_here + jb_here)
    lookup_rows = jnp.concatenate([factor_b, factor_c], 0).reshape(2 * jb_here, BS, R)
    fetched = lax.all_to_all(
        lookup_rows[lax.all_to_all(wanted, "grp", split_axis=0, concat_axis=0, tiled=True)],
        "grp",
        split_axis=0,
        concat_axis=0,
        tiled=True,
    )
    left_rows = fetched[peer_b, slot_b]
    right_rows = fetched[peer_c, slot_c]
    gram_b, gram_c = lax.psum((gram_of(factor_b), gram_of(factor_c)), "grp")
    khatri = (
        left_rows.astype(jnp.float32)[:, :, None, :] * right_rows.astype(jnp.float32)[:, None, :, :]
    )
    khatri = khatri.astype(jnp.bfloat16).reshape(nblk_here, BS * BS, R)
    partial_rows = jnp.einsum("bix,bxr->bir", blocks, khatri, preferred_element_type=jnp.float32)
    peer_a = first_row // part_here
    slot_a = slot_of(peer_a)
    outgoing = jnp.zeros((n_grp, CAP, BS, R), jnp.float32).at[peer_a, slot_a].set(partial_rows)
    target_ids = (
        jnp.zeros((n_grp, CAP), jnp.float32)
        .at[peer_a, slot_a]
        .set((first_row % part_here).astype(jnp.float32))
    )
    arrived, arrived_ids = (
        lax.all_to_all(outgoing, "grp", split_axis=0, concat_axis=0, tiled=True),
        lax.all_to_all(target_ids, "grp", split_axis=0, concat_axis=0, tiled=True),
    )
    dense_rows = jnp.zeros((part_here, BS, R), jnp.float32)
    dense_rows = dense_rows.at[arrived_ids.reshape(-1).astype(jnp.int32)].add(
        arrived.reshape(-1, BS, R)
    )
    mttkrp = lax.psum_scatter(
        dense_rows.reshape(part_here * BS, R), "rep", scatter_dimension=0, tiled=True
    )
    norm_b = jnp.sqrt(jnp.diagonal(gram_b))
    norm_c = jnp.sqrt(jnp.diagonal(gram_c))
    gram = (
        gram_b
        / (norm_b[:, None] * norm_b[None, :])
        * (gram_c / (norm_c[:, None] * norm_c[None, :]))
    )
    target = mttkrp / (norm_b * norm_c)[None, :]

    def sweep(owner_step, factor):
        for within in range(8):
            column = owner_step * 8 + within
            g_column = lax.dynamic_slice_in_dim(gram, column, 1, 1)
            predicted = jnp.dot(factor, g_column, precision=lax.Precision.HIGHEST)
            m_column = lax.dynamic_slice_in_dim(target, column, 1, 1)
            a_column = lax.dynamic_slice_in_dim(factor, column, 1, 1)
            pivot = lax.dynamic_slice_in_dim(g_column, column, 1, 0)
            updated = jnp.maximum(a_column + (m_column - predicted) / pivot, 0.0)
            factor = lax.dynamic_update_slice_in_dim(factor, updated, column, 1)
        return factor

    return lax.fori_loop(0, R // 8, sweep, factor_a)


def solution(mesh):
    placed = (
        P(("grp", "rep"), None, None),
        P(("grp", "rep"), None),
        P(("grp", "rep"), None),
        P("grp", None),
        P("grp", None),
    )
    return jax.shard_map(
        body, mesh=mesh, in_specs=placed, out_specs=P(("grp", "rep"), None), check_vma=False
    )
```

profile of v0, /device:TPU:1, one launch (start us, length us, event | category | flops | bytes accessed | tf_op | source)
XLA Modules:
  0.0 877.7 jit_solution(263737763058058735)
XLA Ops:
  7.4 0.9 fusion.48
  10.9 13.7 %all-to-all-start.1 = ((s32[8,1,4]{2,1,0:T(1,128)}), s32[8,1,4]{2,1,0:T(1,128)S(1)}, u32[]{:S(2)}, u32[]{:S(2)}) async-start(s32[8,1,4]{2,1,0:T(1,128)} %copy.38), calls=%async_computation.1 | async-start | bytes 8192 | tf_op jit(solution)/shard_map/all_to_all | solution.py:42
  24.7 1.1 pad_maximum_fusion
  25.9 3.2 all-to-all-done.1
  29.4 1.4 gather_fusion
  30.8 4.1 all-to-all-start.2
  36.2 0.9 fusion.50
  37.1 7.2 all-to-all-done.2
  44.2 4.2 all-to-all-start
  50.7 0.8 broadcast_in_dim.9
  51.6 1.9 scatter_fusion.3
  53.5 4.8 all-to-all-start.3
  58.3 0.9 fusion.51
  59.4 8.3 all-to-all-done.3
  67.7 2.0 broadcast_in_dim.8
  69.7 2.8 scatter_fusion.4
  72.7 63.6 %all-reduce.3.cloned.1.call-done = (f32[128,128]{1,0:T(8,128)}, f32[128,128]{1,0:T(8,128)}) async-done(((f32[128,128]{1,0:T(8,128)}, f32[128,128]{1,0:T(8,128)}), (f32[128,128]{1,0:T(8,128)}, f32[128,128]{1,0:T(8,128)})) %all-reduce.3.cloned.1.call-update) | async-done | bytes 131088 | tf_op jit(solution)/shard_map/psum | solution.py:50
  136.4 1.9 gather_fusion.3
  138.3 1.9 gather_fusion.4
  140.3 1.0 divide_multiply_fusion
  141.3 609.6 %reduce-scatter.2.cloned.1.call-done = f32[64,128]{1,0:T(8,128)} async-done(((f32[6144,128]{1,0:T(8,128)}), f32[64,128]{1,0:T(8,128)}) %reduce-scatter.2.cloned.1.call-update) | async-done | bytes 32784 | tf_op jit(solution)/shard_map/reduce_scatter | solution.py:72
  751.9 117.7 %while.16 = (s32[]{:T(128)}, f32[64,128]{0,1:T(8,128)S(1)}, f32[64,128]{0,1:T(8,128)S(1)}, f32[128,128]{0,1:T(8,128)S(1)}, s32[]{:T(128)}, /*index=5*/s32[]{:T(1...) while((s32[]{:T(128)}, f32[64,128]{0,1:T(8,128)S(1)}, ...), condition=%wide.region_12.13_spmd, body=%wide.region_11.12_spmd.sunk | while | flops 788522 | bytes 551765 | solution.py:96
  752.6 0.8 fusion.94
  754.3 0.9 fusion.96
  758.4 0.8 fusion.101
  760.0 0.8 fusion.94
  761.6 0.9 fusion.96
  765.7 0.8 fusion.101
  767.3 0.8 fusion.94
  769.0 0.9 fusion.96
  773.1 0.8 fusion.101
  774.7 0.8 fusion.94
  776.3 0.9 fusion.96
  780.4 0.8 fusion.101
  782.1 0.8 fusion.94
  783.7 0.9 fusion.96
  787.8 0.8 fusion.101
  789.4 0.8 fusion.94
  791.1 0.9 fusion.96
  795.2 0.8 fusion.101
  796.8 0.8 fusion.94
  798.4 0.9 fusion.96
  802.5 0.8 fusion.101
  804.1 0.8 fusion.94
  805.8 0.9 fusion.96
  809.9 0.8 fusion.101
  811.5 0.8 fusion.94
  813.1 0.9 fusion.96
  817.2 0.8 fusion.101
  818.9 0.8 fusion.94
  820.5 0.9 fusion.96
  824.6 0.8 fusion.101
  826.2 0.8 fusion.94
  827.8 0.9 fusion.96
  833.6 0.8 fusion.94
  835.2 0.9 fusion.96
  840.9 0.8 fusion.94
  842.6 0.9 fusion.96
  848.3 0.8 fusion.94
  849.9 0.9 fusion.96
  855.6 0.8 fusion.94
  857.3 0.9 fusion.96
  863.0 0.8 fusion.94
  864.6 0.9 fusion.96
  (286 shorter events, 89.2 us)
Async XLA Ops:
  7.4 42.8 %copy-start = (bf16[2,64,4096]{2,1,0:T(8,128)(2,1)S(1)}, bf16[2,64,4096]{2,1,0:T(8,128)(2,1)}, u32[]{:S(2)}) copy-start(bf16[2,64,4096]{2,1,0:T(8,128)(2,1)} %param.7) | copy-start | bytes 3145732
  8.9 27.3 %copy-start.1 = (bf16[1024,128]{1,0:T(8,128)(2,1)S(1)}, bf16[1024,128]{1,0:T(8,128)(2,1)}, u32[]{:S(2)}) copy-start(bf16[1024,128]{1,0:T(8,128)(2,1)} %param.10) | copy-start | bytes 786436
  10.9 18.2 %all-to-all-start.1 = ((s32[8,1,4]{2,1,0:T(1,128)}), s32[8,1,4]{2,1,0:T(1,128)S(1)}, u32[]{:S(2)}, u32[]{:S(2)}) async-start(s32[8,1,4]{2,1,0:T(1,128)} %copy.38), calls=%async_computation.1 | async-start | bytes 8192 | tf_op jit(solution)/shard_map/all_to_all | solution.py:42
  30.8 13.5 %all-to-all-start.2 = ((bf16[8,4,64,128]{3,2,1,0:T(8,128)(2,1)}), bf16[8,4,64,128]{3,2,1,0:T(8,128)(2,1)S(1)}, u32[]{:S(2)}, u32[]{:S(2)}) async-start(bf16[8,4,64,128]{3,2,1,0:T(8,128)(2,1)} %bitcast.52), calls=%async_computation.2 | async-start | bytes 1048576 | tf_op jit(solution)/shard_map/all_to_all | solution.py:41
  44.2 9.3 %all-to-all-start = ((f32[8,1,2]{2,1,0:T(1,128)}), f32[8,1,2]{2,1,0:T(1,128)S(1)}, u32[]{:S(2)}, u32[]{:S(2)}) async-start(f32[8,1,2]{2,1,0:T(1,128)} %copy.35), calls=%async_computation | async-start | bytes 8192 | tf_op jit(solution)/shard_map/all_to_all | solution.py:66
  50.2 8.2 copy-start.2
  53.5 14.2 %all-to-all-start.3 = ((f32[8,2,64,128]{3,2,1,0:T(8,128)}), f32[8,2,64,128]{3,2,1,0:T(8,128)S(1)}, u32[]{:S(2)}, u32[]{:S(2)}) async-start(f32[8,2,64,128]{3,2,1,0:T(8,128)} %scatter_fusion.3), calls=%async_computation.3 | async-start | bytes 1048576 | tf_op jit(solution)/shard_map/all_to_all | solution.py:65
  58.3 78.0 %all-reduce.3.cloned.1.call-start = ((), (), s32[]{:S(2)}) async-start(), calls=%async_computation.6 | async-start | bytes 262144 | tf_op jit(solution)/shard_map/psum | solution.py:50
  59.3 691.7 %reduce-scatter.2.cloned.1.call-start = ((), (), s32[]{:S(2)}) async-start(), calls=%async_computation.5 | async-start | bytes 3178496 | tf_op jit(solution)/shard_map/reduce_scatter | solution.py:72
  69.7 2.9 copy-start.3
Sparse Core Ops, SparseCore 0:
  61.5 74.8 all-reduce.2
Sparse Core Ops, SparseCore 1:
  72.7 678.2 reduce-scatter.1
where the time goes:
time: 880 us; the launch traced here: 878 us
  waiting for transfers between devices  692 us (79%)
  matrix products  103 us (12%)
  local copies, waits for them, and re-layouts  31.7 us (4%)
  starting transfers between devices  26.8 us (3%)
  between operations  15 us (2%)
    reduce_scatter x1, waiting for transfers between devices, body(): lax.psum_scatter(dense_rows.reshape(part_here * BS, R), 'rep', scatter_di...  610 us
    dot_general x128, matrix products, sweep(): predicted = jnp.dot(factor, g_column, precision=lax.Precision.HIGHEST)  101 us
    psum x1, waiting for transfers between devices, body(): gram_b, gram_c = lax.psum((gram_of(factor_b), gram_of(factor_c)), 'grp')  63.6 us
  transfers between devices with their start and end apart: 6, of which 5 were waited for; matrix products, arithmetic and copies ran while one was open for 2% of the time, Pallas kernels for 0%

commit v1 on v0

v1 whole, which is shorter than its diff:
```python
import functools

import jax
import jax.numpy as jnp
from jax import lax
from jax.experimental import pallas as pl
from jax.experimental.pallas import tpu as pltpu
from jax.sharding import PartitionSpec as P

R = 128
BS = 64
CAP = 2
NC = 2
NY = 8
ROWS_Y = 32
MESH = pl.DeviceIdType.MESH


def slot_of(owner):
    count = owner.shape[0]
    same_peer = owner[:, None] == owner[None, :]
    earlier = jnp.arange(count)[None, :] < jnp.arange(count)[:, None]
    return jnp.sum(jnp.logical_and(same_peer, earlier), axis=1)


def gram_of(factor):
    dims = (((0,), (0,)), ((), ()))
    return lax.dot_general(factor, factor, dims, preferred_element_type=jnp.float32)


class Ring:
    def __init__(self, n, me, peer, region, land, send, recv, rows):
        self.n, self.me, self.peer = n, me, peer
        self.region, self.land = region, land
        self.send, self.recv = send, recv
        self.half = n // 2
        self.rows = rows
        self.live = {}

    def at(self, offset):
        return lax.rem(self.me + (offset + 2 * self.n), self.n)

    def span(self, way, step):
        low, high = self.rows
        middle = (low + high) // 2
        if step == 1:
            return (low, middle) if way == 0 else (middle, high)
        return low, high

    def start(self, step):
        for way in (0, 1):
            sign = 1 - 2 * way
            low, high = self.span(way, step)
            copy = pltpu.make_async_remote_copy(
                src_ref=self.region(self.at(sign * (self.half + 1 - step)), low, high),
                dst_ref=self.land(way, step - 1, low, high),
                send_sem=self.send.at[way, step - 1],
                recv_sem=self.recv.at[way, step - 1],
                device_id=self.peer(self.at(sign)),
                device_id_type=MESH,
            )
            copy.start()
            self.live[way, step] = copy

    def finish(self, step):
        for way in (0, 1):
            sign = 1 - 2 * way
            low, high = self.span(way, step)
            self.live[way, step].wait_recv()
            mine = self.region(self.at(sign * (self.half - step)), low, high)
            mine[...] = mine[...] + self.land(way, step - 1, low, high)[...]

    def drain(self):
        for copy in self.live.values():
            copy.wait_send()


def exchange_kernel(
    n_x, n_z, load_ref, gram_ref, out_ref, gsum_ref,
    held, dense, gbuf, land_y, land_x, land_x2, land_y2,
    zs, zr, cs, cr, gs, gr, ys, yr, xs, xr, x2s, x2r, y2s, y2r,
):
    grp, rep = lax.axis_index("grp"), lax.axis_index("rep")
    n_grp = n_x * NC
    my_x, my_c = grp // NC, lax.rem(grp, NC)
    my_z, my_y = rep // NY, lax.rem(rep, NY)
    half_z = n_z // 2

    def z_at(offset):
        return lax.rem(my_z + (offset + 2 * n_z), n_z)

    def z_peer(z):
        return {"grp": grp, "rep": z * NY + my_y}

    def y_peer(y):
        return {"grp": grp, "rep": my_z * NY + y}

    def x_peer(x):
        return {"grp": x * NC + my_c, "rep": rep}

    def grp_peer(g):
        return {"grp": g, "rep": rep}

    barrier = pltpu.get_barrier_semaphore()
    greeted = [z_peer(z_at(1)), z_peer(z_at(-1))]
    greeted += [y_peer(lax.rem(my_y + 1, NY)), y_peer(lax.rem(my_y + NY - 1, NY))]
    greeted += [grp_peer(lax.rem(grp + k, n_grp)) for k in range(1, n_grp)]
    for who in greeted:
        pl.semaphore_signal(barrier, inc=1, device_id=who, device_id_type=MESH)
    pl.semaphore_wait(barrier, len(greeted))

    def remote(src, dst, send, recv, who):
        copy = pltpu.make_async_remote_copy(
            src_ref=src, dst_ref=dst, send_sem=send, recv_sem=recv,
            device_id=who, device_id_type=MESH,
        )
        copy.start()
        return copy

    sent = []
    partner = grp_peer(my_x * NC + (1 - my_c))
    z_live, c_live = {}, {}

    def pass_on(step, way, piece):
        origin = z_at(-(step - 1) if way == 0 else step - 1)
        src = load_ref.at[piece] if step == 1 else held.at[origin, my_c, piece]
        copy = remote(
            src, held.at[origin, my_c, piece],
            zs.at[way, step - 1, piece], zr.at[way, step - 1, piece],
            z_peer(z_at(1 if way == 0 else -1)),
        )
        z_live[step, way, piece] = copy
        sent.append(copy)

    def hand_over(offset, piece):
        origin = z_at(offset)
        src = load_ref.at[piece] if offset == 0 else held.at[origin, my_c, piece]
        slot = offset + half_z
        copy = remote(
            src, held.at[origin, my_c, piece], cs.at[slot, piece], cr.at[slot, piece], partner
        )
        c_live[offset, piece] = copy
        sent.append(copy)

    for piece in range(2):
        for way in range(2):
            if 1 < half_z or piece == way:
                pass_on(1, way, piece)
    for piece in range(2):
        hand_over(0, piece)
    gram_live = []
    for k in range(1, n_grp):
        copy = remote(
            gram_ref, gbuf.at[grp], gs.at[k - 1], gr.at[k - 1],
            grp_peer(lax.rem(grp + k, n_grp)),
        )
        gram_live.append(copy)
        sent.append(copy)
    gbuf[grp] = gram_ref[...]
    for piece in range(2):
        held[my_z, my_c, piece] = load_ref[piece]

    def absorb(offset, first):
        origin = z_at(offset)
        marks = [held[origin, c, b, BS : BS + 8, :] for c in range(NC) for b in range(2)]
        for part in range(2):
            rows = slice(part * (BS // 2), (part + 1) * (BS // 2))
            parts = [held[origin, c, b, rows, :] for c in range(NC) for b in range(2)]

            def place(slot, carry):
                x, y = slot // NY, lax.rem(slot, NY)
                target = ((x * NC + my_c) * (n_z * NY) + my_z * NY + y).astype(jnp.float32)
                total = None if first else dense[x, y, rows, :]
                for mark, block in zip(marks, parts):
                    hit = jnp.concatenate([mark == target] * (BS // 16), axis=0)
                    term = jnp.where(hit, block, 0.0)
                    total = term if total is None else total + term
                dense[x, y, rows, :] = total
                return carry

            lax.fori_loop(0, n_x * NY, place, 0)

    def carried(step, way, piece):
        return step < half_z or piece == way

    waiting = [0]
    fresh = True
    for step in range(1, half_z + 1):
        arrived = []
        for offset in waiting:
            for piece in range(2):
                c_live[offset, piece].wait_recv()
            absorb(offset, fresh)
            fresh = False
        for piece in range(2):
            for way in range(2):
                if carried(step, way, piece):
                    z_live[step, way, piece].wait_recv()
                    if step < half_z and carried(step + 1, way, piece):
                        pass_on(step + 1, way, piece)
                    offset = -step if way == 0 else step
                    if step == half_z:
                        offset = -step
                    hand_over(offset, piece)
                    if offset not in arrived:
                        arrived.append(offset)
        waiting = arrived
    for offset in waiting:
        for piece in range(2):
            c_live[offset, piece].wait_recv()
        absorb(offset, fresh)

    y_first = Ring(
        NY, my_y, y_peer,
        lambda y, low, high: dense.at[:, y, low:high, :],
        lambda way, step, low, high: land_y.at[way, step, :, low:high, :],
        ys, yr, (0, ROWS_Y),
    )
    x_first = Ring(
        n_x, my_x, x_peer,
        lambda x, low, high: dense.at[x, :, low:high, :],
        lambda way, step, low, high: land_x.at[way, step, :, low - ROWS_Y : high - ROWS_Y, :],
        xs, xr, (ROWS_Y, BS),
    )
    x_last = Ring(
        n_x, my_x, x_peer,
        lambda x, low, high: dense.at[x, my_y, low:high, :],
        lambda way, step, low, high: land_x2.at[way, step, low:high, :],
        x2s, x2r, (0, ROWS_Y),
    )
    y_last = Ring(
        NY, my_y, y_peer,
        lambda y, low, high: dense.at[my_x, y, low:high, :],
        lambda way, step, low, high: land_y2.at[way, step, low - ROWS_Y : high - ROWS_Y, :],
        y2s, y2r, (ROWS_Y, BS),
    )

    def stages(first, second):
        yield lambda: first.start(1)
        for step in range(1, first.half + 1):
            def turn(step=step):
                first.finish(step)
                if step < first.half:
                    first.start(step + 1)
                else:
                    second.start(1)
            yield turn
        for step in range(1, second.half + 1):
            def turn(step=step):
                second.finish(step)
                if step < second.half:
                    second.start(step + 1)
            yield turn

    chain_y, chain_x = list(stages(y_first, x_last)), list(stages(x_first, y_last))
    for index in range(max(len(chain_y), len(chain_x))):
        for chain in (chain_y, chain_x):
            if index < len(chain):
                chain[index]()
        if index == 0:
            for copy in gram_live:
                copy.wait_recv()
            gsum_ref[...] = functools.reduce(lambda a, b: a + b, [gbuf[g] for g in range(n_grp)])
    out_ref[...] = dense[my_x, my_y]
    for copy in sent:
        copy.wait_send()
    for ring in (y_first, x_first, x_last, y_last):
        ring.drain()


def exchange(load, gram, n_x, n_z):
    half_z, half_y, half_x = n_z // 2, NY // 2, n_x // 2
    vmem = pl.BlockSpec(memory_space=pltpu.VMEM)
    dma = pltpu.SemaphoreType.DMA
    rest = BS - ROWS_Y
    return pl.pallas_call(
        functools.partial(exchange_kernel, n_x, n_z),
        out_shape=(
            jax.ShapeDtypeStruct((BS, R), jnp.float32),
            jax.ShapeDtypeStruct((2 * R, R), jnp.float32),
        ),
        in_specs=[vmem, vmem],
        out_specs=(vmem, vmem),
        scratch_shapes=[
            pltpu.VMEM((n_z, NC, 2, BS + 8, R), jnp.float32),
            pltpu.VMEM((n_x, NY, BS, R), jnp.float32),
            pltpu.VMEM((n_x * NC, 2 * R, R), jnp.float32),
            pltpu.VMEM((2, half_y, n_x, ROWS_Y, R), jnp.float32),
            pltpu.VMEM((2, half_x, NY, rest, R), jnp.float32),
            pltpu.VMEM((2, half_x, ROWS_Y, R), jnp.float32),
            pltpu.VMEM((2, half_y, rest, R), jnp.float32),
            dma((2, half_z, 2)), dma((2, half_z, 2)),
            dma((n_z + 1, 2)), dma((n_z + 1, 2)),
            dma((n_x * NC - 1,)), dma((n_x * NC - 1,)),
            dma((2, half_y)), dma((2, half_y)),
            dma((2, half_x)), dma((2, half_x)),
            dma((2, half_x)), dma((2, half_x)),
            dma((2, half_y)), dma((2, half_y)),
        ],
        compiler_params=pltpu.CompilerParams(collective_id=0, has_side_effects=True),
        name="exchange",
    )(load, gram)


def sweep_kernel(m_ref, a_ref, g_ref, out_ref):
    gram_b, gram_c = g_ref[0:R, :], g_ref[R : 2 * R, :]
    down = lax.broadcasted_iota(jnp.int32, (R, R), 0)
    across = lax.broadcasted_iota(jnp.int32, (R, R), 1)
    on_diag = down == across

    def diagonals(square):
        kept = jnp.where(on_diag, square, 0.0)
        return jnp.sum(kept, axis=0, keepdims=True), jnp.sum(kept, axis=1, keepdims=True)

    b_row, b_col = diagonals(gram_b)
    c_row, c_col = diagonals(gram_c)
    b_row, b_col = jnp.sqrt(b_row), jnp.sqrt(b_col)
    c_row, c_col = jnp.sqrt(c_row), jnp.sqrt(c_col)
    gram = gram_b / (b_col * b_row) * (gram_c / (c_col * c_row))
    target = m_ref[...] / (b_row * c_row)
    pivot_row, pivot_col = diagonals(gram)
    later = jnp.where(down > across, gram, 0.0)
    known = jnp.dot(
        a_ref[...], later, precision=lax.Precision.HIGHEST, preferred_element_type=jnp.float32
    )
    start = ((target - known) / pivot_row).T
    weight = jnp.where(down > across, gram / pivot_col, 0.0)
    tiles = [start[8 * k : 8 * k + 8, :] for k in range(R // 8)]
    weights = [weight[8 * k : 8 * k + 8, :] for k in range(R // 8)]
    for r in range(R):
        own, sub = r // 8, r % 8
        fixed = jnp.maximum(jnp.broadcast_to(tiles[own][sub : sub + 1, :], (8, BS)), 0.0)
        for k in range(own, R // 8):
            if k == own and sub == 7:
                continue
            scale = jnp.broadcast_to(weights[k][:, r : r + 1], (8, BS))
            tiles[k] = tiles[k] - scale * fixed
    out_ref[...] = jnp.maximum(jnp.concatenate(tiles, axis=0), 0.0).T


def sweep(mttkrp, factor_a, gram):
    vmem = pl.BlockSpec(memory_space=pltpu.VMEM)
    return pl.pallas_call(
        sweep_kernel,
        out_shape=jax.ShapeDtypeStruct((BS, R), jnp.float32),
        in_specs=[vmem] * 3,
        out_specs=vmem,
        name="sweep",
    )(mttkrp, factor_a, gram)


def body(blocks, coords, factor_a, factor_b, factor_c):
    n_grp = lax.axis_size("grp")
    n_rep = lax.axis_size("rep")
    nblk_here = blocks.shape[0]
    jb_here = factor_b.shape[0] // BS
    first_row = coords[:, 0]
    second_row = coords[:, 1]
    third_row = coords[:, 2]
    peer_b = second_row // jb_here
    peer_c = third_row // jb_here
    slot_b = slot_of(peer_b)
    slot_c = slot_of(peer_c) + CAP
    wanted = jnp.zeros((n_grp, 2 * CAP), jnp.int32)
    wanted = wanted.at[peer_b, slot_b].set(second_row % jb_here)
    wanted = wanted.at[peer_c, slot_c].set(third_row % jb_here + jb_here)
    lookup_rows = jnp.concatenate([factor_b, factor_c], 0).reshape(2 * jb_here, BS, R)
    fetched = lax.all_to_all(
        lookup_rows[lax.all_to_all(wanted, "grp", split_axis=0, concat_axis=0, tiled=True)],
        "grp",
        split_axis=0,
        concat_axis=0,
        tiled=True,
    )
    left_rows = fetched[peer_b, slot_b]
    right_rows = fetched[peer_c, slot_c]
    gram_part = jnp.concatenate([gram_of(factor_b), gram_of(factor_c)], 0)
    khatri = (
        left_rows.astype(jnp.float32)[:, :, None, :] * right_rows.astype(jnp.float32)[:, None, :, :]
    )
    khatri = khatri.astype(jnp.bfloat16).reshape(nblk_here, BS * BS, R)
    partial_rows = jnp.einsum("bix,bxr->bir", blocks, khatri, preferred_element_type=jnp.float32)
    marks = jnp.broadcast_to(first_row.astype(jnp.float32)[:, None, None], (nblk_here, 8, R))
    load = jnp.concatenate([partial_rows, marks], 1)
    mttkrp, gram = exchange(load, gram_part, n_grp // NC, n_rep // NY)
    return sweep(mttkrp, factor_a, gram)


def solution(mesh):
    placed = (
        P(("grp", "rep"), None, None),
        P(("grp", "rep"), None),
        P(("grp", "rep"), None),
        P("grp", None),
        P("grp", None),
    )
    return jax.shard_map(
        body, mesh=mesh, in_specs=placed, out_specs=P(("grp", "rep"), None), check_vma=False
    )
```

time: 880 us -> 99 us (0.11)
  the two profiles are of different devices: /device:TPU:1 before, /device:TPU:24 now
where the time goes in v1:
time: 99 us; the launch traced here: 98.7 us
  Pallas kernels  67.2 us (68%)
  waiting for transfers between devices  14.1 us (14%)
  starting transfers between devices  7.79 us (8%)
  local copies, waits for them, and re-layouts  5.87 us (6%)
  other arithmetic  2.54 us (3%)
  matrix products  1.03 us (1%)
    pallas_call x1, Pallas kernels, exchange(): pl.pallas_call(functools.partial(exchange_kernel, n_x, n_z), out_shape=(j...  63.9 us
    all_to_all x1, waiting for transfers between devices, body(): lax.all_to_all(lookup_rows[lax.all_to_all(wanted, 'grp', split_axis=0, co...  9.18 us
    all_to_all x1, waiting for transfers between devices, body(): lax.all_to_all(wanted, 'grp', split_axis=0, concat_axis=0, tiled=True)  4.89 us
    all_to_all x1, starting transfers between devices, body(): lax.all_to_all(wanted, 'grp', split_axis=0, concat_axis=0, tiled=True)  4.3 us
    all_to_all x1, starting transfers between devices, body(): lax.all_to_all(lookup_rows[lax.all_to_all(wanted, 'grp', split_axis=0, co...  3.49 us
    pallas_call x1, Pallas kernels, sweep(): pl.pallas_call(sweep_kernel, out_shape=jax.ShapeDtypeStruct((BS, R), jnp....  3.29 us
  transfers between devices with their start and end apart: 2, of which 2 were waited for; matrix products, arithmetic and copies ran while one was open for 1% of the time, Pallas kernels for 0%

profile of v1, /device:TPU:24, one launch (start us, length us, event | category | flops | bytes accessed | tf_op | source)
XLA Modules:
  0.0 98.7 jit_solution(17639854582351759223)
XLA Ops:
  0.0 0.0 copy-start
  0.0 0.0 copy-start.1
  0.0 0.0 copy-start.2
  0.0 0.9 fusion.9
  0.9 0.1 copy.22
  1.0 0.1 copy.23
  1.1 0.2 fusion
  1.3 0.2 fusion.1
  1.6 0.6 scatter_fusion
  2.2 0.6 scatter_fusion.1
  2.8 0.0 copy-start.3
  2.8 0.7 copy.19
  3.5 4.3 %all-to-all-start = ((s32[8,1,4]{2,1,0:T(1,128)}), s32[8,1,4]{2,1,0:T(1,128)S(1)}, u32[]{:S(2)}, u32[]{:S(2)}) async-start(s32[8,1,4]{2,1,0:T(1,128)} %copy.19), calls=%async_computation | async-start | bytes 8192 | tf_op jit(solution)/shard_map/all_to_all | solution.py:369
  7.8 0.0 copy-done.1
  7.8 0.3 fusion.10
  8.1 0.0 copy-done.2
  8.1 4.9 %all-to-all-done = s32[8,1,4]{2,1,0:T(1,128)S(1)} async-done(((s32[8,1,4]{2,1,0:T(1,128)}), s32[8,1,4]{2,1,0:T(1,128)S(1)}, u32[]{:S(2)}, u32[]{:S(2)}) %all-to-all-start) | async-done | bytes 160 | tf_op jit(solution)/shard_map/all_to_all | solution.py:369
  13.0 0.1 copy.20
  13.1 0.1 copy.21
  13.2 0.1 reshape.142
  13.3 1.4 %gather_fusion = bf16[32,64,128]{2,1,0:T(8,128)(2,1)} fusion(bf16[32,64,128]{2,1,0:T(8,128)(2,1)S(1)} %bitcast.79, s32[1024]{0:T(1024)S(1)} %pad_clamp_fusion), kind=kCustom, calls=%fused_computation | custom fusion | bytes 1048704 | tf_op jit(solution)/shard_map/gather | solution.py:369
  14.7 3.5 %all-to-all-start.1 = ((bf16[8,4,64,128]{3,2,1,0:T(8,128)(2,1)}), bf16[8,4,64,128]{3,2,1,0:T(8,128)(2,1)S(1)}, u32[]{:S(2)}, u32[]{:S(2)}) async-start(bf16[8,4,64,128]{3,2,1,0:T(8,128)(2,1)} %bitcast.12), calls=%async_computation.1 | async-start | bytes 1048576 | tf_op jit(solution)/shard_map/all_to_all | solution.py:368
  18.2 0.0 copy-done.3
  18.2 0.1 convert_reduce_fusion
  18.3 0.3 fusion.11
  18.6 0.7 pad_maximum_fusion.1.gram_ref
  19.2 9.2 %all-to-all-done.1 = bf16[8,4,64,128]{3,2,1,0:T(8,128)(2,1)S(1)} async-done(((bf16[8,4,64,128]{3,2,1,0:T(8,128)(2,1)}), bf16[8,4,64,128]{3,2,1,0:T(8,128)(2,1)S(1)}, u32[]{:S(2)}, u32[]{:S(2)}) %all-to-all-start.1) | async-done | bytes 524320 | tf_op jit(solution)/shard_map/all_to_all | solution.py:368
  28.4 0.6 gather_fusion.1
  29.0 0.6 gather_fusion.2
  29.6 0.6 multiply_convert_fusion
  30.2 0.0 copy-done
  30.2 0.5 convolution_bitcast_fusion
  30.7 0.1 broadcast_in_dim.2
  30.8 0.6 pad_maximum_fusion.2.load_ref
  31.4 63.9 %exchange.1 = (f32[64,128]{1,0:T(8,128)}, f32[256,128]{1,0:T(8,128)}) custom-call(f32[2,72,128]{2,1,0:T(8,128)} %pad_maximum_fusion.2.load_ref, f32[256,128]{1,0:T(8,128)} %pad_maximum_fusion.1.gram_ref), custom_call_target="tpu_custom_call" | custom-call | tf_op jit(solution)/shard_map/exchange/pallas_call | solution.py:276
  95.4 3.3 %sweep.1 = f32[64,128]{1,0:T(8,128)} custom-call(f32[64,128]{1,0:T(8,128)} %get-tuple-element.7.m_ref, f32[64,128]{1,0:T(8,128)} %a_ref.1, f32[256,128]{1,0:T(8,128)} %get-tuple-element.8.g_ref), custom_call_target="tpu_custom_call" | custom-call | tf_op jit(solution)/shard_map/sweep/pallas_call | solution.py:343
  (12 shorter events, 0.1 us)
Async XLA Ops:
  0.0 30.2 %copy-start = (bf16[2,64,4096]{2,1,0:T(8,128)(2,1)S(1)}, bf16[2,64,4096]{2,1,0:T(8,128)(2,1)}, u32[]{:S(2)}) copy-start(bf16[2,64,4096]{2,1,0:T(8,128)(2,1)} %param.5) | copy-start | bytes 3145732
  0.0 7.8 %copy-start.1 = (bf16[1024,128]{1,0:T(8,128)(2,1)S(1)}, bf16[1024,128]{1,0:T(8,128)(2,1)}, u32[]{:S(2)}) copy-start(bf16[1024,128]{1,0:T(8,128)(2,1)} %param.8) | copy-start | bytes 786436
  0.0 8.1 %copy-start.2 = (bf16[1024,128]{1,0:T(8,128)(2,1)S(1)}, bf16[1024,128]{1,0:T(8,128)(2,1)}, u32[]{:S(2)}) copy-start(bf16[1024,128]{1,0:T(8,128)(2,1)} %param.9) | copy-start | bytes 786436
  2.8 15.4 %copy-start.3 = (s32[2,3]{1,0:T(2,128)S(1)}, s32[2,3]{1,0:T(2,128)}, u32[]{:S(2)}) copy-start(s32[2,3]{1,0:T(2,128)} %param.6) | copy-start | bytes 76
  3.5 9.5 %all-to-all-start = ((s32[8,1,4]{2,1,0:T(1,128)}), s32[8,1,4]{2,1,0:T(1,128)S(1)}, u32[]{:S(2)}, u32[]{:S(2)}) async-start(s32[8,1,4]{2,1,0:T(1,128)} %copy.19), calls=%async_computation | async-start | bytes 8192 | tf_op jit(solution)/shard_map/all_to_all | solution.py:369
  14.7 13.7 %all-to-all-start.1 = ((bf16[8,4,64,128]{3,2,1,0:T(8,128)(2,1)}), bf16[8,4,64,128]{3,2,1,0:T(8,128)(2,1)S(1)}, u32[]{:S(2)}, u32[]{:S(2)}) async-start(bf16[8,4,64,128]{3,2,1,0:T(8,128)(2,1)} %bitcast.12), calls=%async_computation.1 | async-start | bytes 1048576 | tf_op jit(solution)/shard_map/all_to_all | solution.py:368

commit v2 on v1

v2 whole, which is shorter than its diff:
```python
import functools

import jax
import jax.numpy as jnp
from jax import lax
from jax.experimental import pallas as pl
from jax.experimental.pallas import tpu as pltpu
from jax.sharding import PartitionSpec as P

R = 128
BS = 64
NC = 2
NY = 8
ROWS_Y = 24
MESH = pl.DeviceIdType.MESH


class Ring:
    def __init__(self, n, me, peer, region, land, send, recv, rows):
        self.n, self.me, self.peer = n, me, peer
        self.region, self.land = region, land
        self.send, self.recv = send, recv
        self.half = n // 2
        self.rows = rows
        self.live = {}

    def at(self, offset):
        return lax.rem(self.me + (offset + 2 * self.n), self.n)

    def span(self, way, step):
        low, high = self.rows
        middle = low + (high - low) // 16 * 8
        if step == 1:
            return (low, middle) if way == 0 else (middle, high)
        return low, high

    def start(self, step):
        for way in (0, 1):
            sign = 1 - 2 * way
            low, high = self.span(way, step)
            copy = pltpu.make_async_remote_copy(
                src_ref=self.region(self.at(sign * (self.half + 1 - step)), low, high),
                dst_ref=self.land(way, step - 1, low, high),
                send_sem=self.send.at[way, step - 1],
                recv_sem=self.recv.at[way, step - 1],
                device_id=self.peer(self.at(sign)),
                device_id_type=MESH,
            )
            copy.start()
            self.live[way, step] = copy

    def finish(self, step):
        for way in (0, 1):
            sign = 1 - 2 * way
            low, high = self.span(way, step)
            self.live[way, step].wait_recv()
            mine = self.region(self.at(sign * (self.half - step)), low, high)
            mine[...] = mine[...] + self.land(way, step - 1, low, high)[...]

    def drain(self):
        for copy in self.live.values():
            copy.wait_send()


def update_kernel(
    n_x, n_z, coords_ref, coords_sm, blocks_ref, b_ref, c_ref, out_ref, gsum_ref,
    cbuf, blocks, table, picked, rows_in, khatri, load, held, dense,
    gpart, gbuf, gfin, land_y, land_x, land_x2, land_y2, part_y, part_x,
    local, ks, kr, ts, tr, fs, fr, zs, zr, cs, cr, gs, gr, hs, hr,
    ys, yr, xs, xr, x2s, x2r, y2s, y2r,
):
    grp, rep = lax.axis_index("grp"), lax.axis_index("rep")
    n_grp = n_x * NC
    my_x, my_c = grp // NC, lax.rem(grp, NC)
    my_z, my_y = rep // NY, lax.rem(rep, NY)
    half_z = n_z // 2
    jblocks = b_ref.shape[0]
    chip_blocks = NC * jblocks

    def z_at(offset):
        return lax.rem(my_z + (offset + 2 * n_z), n_z)

    def z_peer(offset):
        return {"grp": grp, "rep": z_at(offset) * NY + my_y}

    def y_peer(y):
        return {"grp": grp, "rep": my_z * NY + y}

    def x_peer(x):
        return {"grp": x * NC + my_c, "rep": rep}

    def grp_peer(g):
        return {"grp": g, "rep": rep}

    partner = grp_peer(my_x * NC + (1 - my_c))
    own_rows = pl.ds(my_c * jblocks, jblocks)
    fetch_blocks = pltpu.make_async_copy(blocks_ref, blocks, local.at[0])
    fetch_blocks.start()

    @pl.when(my_c == 0)
    def _():
        pltpu.make_async_copy(b_ref, table.at[own_rows], local.at[1]).start()

    @pl.when(my_c != 0)
    def _():
        pltpu.make_async_copy(c_ref, table.at[own_rows], local.at[1]).start()

    barrier = pltpu.get_barrier_semaphore()
    greeted = [grp_peer(lax.rem(grp + k, n_grp)) for k in range(1, n_grp)]
    greeted += [y_peer(lax.rem(my_y + k, NY)) for k in range(1, NY)]
    greeted += [z_peer(k) for k in (1, -1, 2, -2)]
    for who in greeted:
        pl.semaphore_signal(barrier, inc=1, device_id=who, device_id_type=MESH)
    pl.semaphore_wait(barrier, len(greeted))

    sent = []

    def remote(src, dst, send, recv, who):
        copy = pltpu.make_async_remote_copy(
            src_ref=src, dst_ref=dst, send_sem=send, recv_sem=recv,
            device_id=who, device_id_type=MESH,
        )
        copy.start()
        sent.append(copy)
        return copy

    asked = [
        remote(
            coords_ref, cbuf.at[grp], ks.at[k - 1], kr.at[k - 1],
            grp_peer(lax.rem(grp + k, n_grp)),
        )
        for k in range(1, n_grp)
    ]

    def share(ref):
        return pltpu.make_async_remote_copy(
            src_ref=ref, dst_ref=table.at[own_rows], send_sem=ts, recv_sem=tr,
            device_id=partner, device_id_type=MESH,
        )

    @pl.when(my_c == 0)
    def _():
        share(c_ref).start()

    @pl.when(my_c != 0)
    def _():
        share(b_ref).start()

    pltpu.make_async_copy(b_ref, table.at[own_rows], local.at[1]).wait()
    sent.append(share(b_ref))
    share(b_ref).wait_recv()

    def look_up(q):
        return table[lax.rem(q, chip_blocks)]

    answered = []
    for k in range(1, n_grp):
        asked[k - 1].wait_recv()
        asker = lax.rem(grp + (n_grp - k), n_grp)
        for b in range(2):
            picked[k - 1, b] = look_up(cbuf[asker, b, 1 + my_c])
        answered.append(
            remote(
                picked.at[k - 1], rows_in.at[my_x, my_c], fs.at[k - 1], fr.at[k - 1],
                grp_peer(asker),
            )
        )
    for b in range(2):
        rows_in[my_x, my_c, b] = look_up(coords_sm[b, 1 + my_c])

    dims = (((0,), (0,)), ((), ()))
    whole = table[...].reshape(chip_blocks * BS, R)
    gpart[...] = lax.dot_general(whole, whole, dims, preferred_element_type=jnp.float32)
    fetch_blocks.wait()
    for copy in answered:
        copy.wait_recv()

    z_live, c_live = {}, {}

    def carried(distance, way, piece):
        return distance < half_z or piece == way

    def pass_on(distance, way, piece):
        sign = 1 if way == 0 else -1
        hop = min(distance, 2)
        origin = z_at(-sign * (distance - hop))
        src = load.at[piece] if distance <= 2 else held.at[origin, my_c, piece]
        z_live[distance, way, piece] = remote(
            src, held.at[origin, my_c, piece],
            zs.at[way, distance - 1, piece], zr.at[way, distance - 1, piece],
            z_peer(sign * hop),
        )

    def hand_over(offset, piece):
        origin = z_at(offset)
        src = load.at[piece] if offset == 0 else held.at[origin, my_c, piece]
        slot = offset + half_z
        c_live[offset, piece] = remote(
            src, held.at[origin, my_c, piece], cs.at[slot, piece], cr.at[slot, piece], partner
        )

    for piece in range(2):
        left = rows_in[lax.div(coords_sm[piece, 1], chip_blocks), 0, piece].astype(jnp.float32)
        right = rows_in[lax.div(coords_sm[piece, 2], chip_blocks), 1, piece].astype(jnp.float32)
        for j in range(BS):
            khatri[j * BS : (j + 1) * BS, :] = (left[j : j + 1, :] * right).astype(jnp.bfloat16)
        partial = jnp.dot(blocks[piece], khatri[...], preferred_element_type=jnp.float32)
        mark = jnp.full((8, R), coords_sm[piece, 0], jnp.int32).astype(jnp.float32)
        load[piece, 0:BS, :] = partial
        load[piece, BS : BS + 8, :] = mark
        for distance in (2, 1):
            for way in range(2):
                if distance <= half_z and carried(distance, way, piece):
                    pass_on(distance, way, piece)
        hand_over(0, piece)
        held[my_z, my_c, piece, 0:BS, :] = partial
        held[my_z, my_c, piece, BS : BS + 8, :] = mark

    gram_live = [
        remote(
            gpart, gbuf.at[my_x], gs.at[k - 1], gr.at[k - 1], x_peer(lax.rem(my_x + k, n_x))
        )
        for k in range(1, n_x)
    ]
    gbuf[my_x] = gpart[...]

    def absorb(offset, first):
        origin = z_at(offset)
        marks = [held[origin, c, b, BS : BS + 8, :] for c in range(NC) for b in range(2)]
        for part in range(2):
            rows = slice(part * (BS // 2), (part + 1) * (BS // 2))
            parts = [held[origin, c, b, rows, :] for c in range(NC) for b in range(2)]

            def place(slot, carry):
                x, y = slot // NY, lax.rem(slot, NY)
                target = ((x * NC + my_c) * (n_z * NY) + my_z * NY + y).astype(jnp.float32)
                total = None if first else dense[x, y, rows, :]
                for mark, block in zip(marks, parts):
                    hit = jnp.concatenate([mark == target] * (BS // 16), axis=0)
                    term = jnp.where(hit, block, 0.0)
                    total = term if total is None else total + term
                dense[x, y, rows, :] = total
                return carry

            lax.fori_loop(0, n_x * NY, place, 0)

    waiting = [0]
    fresh = True
    for distance in range(1, half_z + 1):
        arrived = []
        for offset in waiting:
            for piece in range(2):
                c_live[offset, piece].wait_recv()
            absorb(offset, fresh)
            fresh = False
        for piece in range(2):
            for way in range(2):
                if not carried(distance, way, piece):
                    continue
                z_live[distance, way, piece].wait_recv()
                onward = distance + 2
                if onward <= half_z and carried(onward, way, piece):
                    pass_on(onward, way, piece)
                offset = -distance if way == 0 or distance == half_z else distance
                hand_over(offset, piece)
                if offset not in arrived:
                    arrived.append(offset)
        waiting = arrived
    for offset in waiting:
        for piece in range(2):
            c_live[offset, piece].wait_recv()
        absorb(offset, fresh)

    def spread(n, me, peer, source, land, send, recv):
        order = sorted(range(1, n), key=lambda k: -min(k, n - k))
        live = []
        for k in order:
            to = lax.rem(me + k, n)
            live.append(remote(source(to), land.at[k - 1], send.at[k - 1], recv.at[k - 1], peer(to)))
        return live

    y_first = spread(
        NY, my_y, y_peer, lambda y: dense.at[:, y, 0:ROWS_Y, :], land_y, ys, yr
    )
    x_first = Ring(
        n_x, my_x, x_peer,
        lambda x, low, high: dense.at[x, :, low:high, :],
        lambda way, step, low, high: land_x.at[way, step, :, low - ROWS_Y : high - ROWS_Y, :],
        xs, xr, (ROWS_Y, BS),
    )
    x_first.start(1)
    for copy in gram_live:
        copy.wait_recv()
    gram = gbuf[0]
    for x in range(1, n_x):
        gram = gram + gbuf[x]
    gsum_ref[my_c] = gram
    gpart_all = gfin.at[0]
    gpart_all[...] = gram
    gram_over = remote(gpart_all, gfin.at[1], hs, hr, partner)
    for step in range(1, x_first.half):
        x_first.finish(step)
        x_first.start(step + 1)
    x_first.finish(x_first.half)
    part_x[...] = dense[my_x, :, ROWS_Y:BS, :]
    y_last = spread(NY, my_y, y_peer, lambda y: part_x.at[y], land_y2, y2s, y2r)
    for copy in y_first:
        copy.wait_recv()
    for x in range(n_x):
        total = dense[x, my_y, 0:ROWS_Y, :]
        for k in range(NY - 1):
            total = total + land_y[k, x]
        part_y[x] = total
    x_last = spread(n_x, my_x, x_peer, lambda x: part_y.at[x], land_x2, x2s, x2r)
    gram_over.wait_recv()
    gsum_ref[1 - my_c] = gfin[1]
    for copy in x_last:
        copy.wait_recv()
    total = part_y[my_x]
    for k in range(n_x - 1):
        total = total + land_x2[k]
    out_ref[0:ROWS_Y, :] = total
    for copy in y_last:
        copy.wait_recv()
    total = part_x[my_y]
    for k in range(NY - 1):
        total = total + land_y2[k]
    out_ref[ROWS_Y:BS, :] = total
    for copy in sent:
        copy.wait_send()
    x_first.drain()


def update(coords, blocks, factor_b, factor_c, n_x, n_z):
    half_z, half_x, n_grp = n_z // 2, n_x // 2, n_x * NC
    vmem = pl.BlockSpec(memory_space=pltpu.VMEM)
    anywhere = pl.BlockSpec(memory_space=pl.ANY)
    dma = pltpu.SemaphoreType.DMA
    rest = BS - ROWS_Y
    f32, bf16 = jnp.float32, jnp.bfloat16
    factor_b, factor_c = factor_b.reshape(-1, BS, R), factor_c.reshape(-1, BS, R)
    jblocks = factor_b.shape[0]
    return pl.pallas_call(
        functools.partial(update_kernel, n_x, n_z),
        out_shape=(
            jax.ShapeDtypeStruct((BS, R), f32),
            jax.ShapeDtypeStruct((2, R, R), f32),
        ),
        in_specs=[vmem, pl.BlockSpec(memory_space=pltpu.SMEM), anywhere, anywhere, anywhere],
        out_specs=(vmem, vmem),
        scratch_shapes=[
            pltpu.SMEM((n_grp,) + coords.shape, jnp.int32),
            pltpu.VMEM(blocks.shape, bf16),
            pltpu.VMEM((NC * jblocks, BS, R), bf16),
            pltpu.VMEM((n_grp - 1, 2, BS, R), bf16),
            pltpu.VMEM((n_x, NC, 2, BS, R), bf16),
            pltpu.VMEM((BS * BS, R), bf16),
            pltpu.VMEM((2, BS + 8, R), f32),
            pltpu.VMEM((n_z, NC, 2, BS + 8, R), f32),
            pltpu.VMEM((n_x, NY, BS, R), f32),
            pltpu.VMEM((R, R), f32),
            pltpu.VMEM((n_x, R, R), f32),
            pltpu.VMEM((2, R, R), f32),
            pltpu.VMEM((NY - 1, n_x, ROWS_Y, R), f32),
            pltpu.VMEM((2, half_x, NY, rest, R), f32),
            pltpu.VMEM((n_x - 1, ROWS_Y, R), f32),
            pltpu.VMEM((NY - 1, rest, R), f32),
            pltpu.VMEM((n_x, ROWS_Y, R), f32),
            pltpu.VMEM((NY, rest, R), f32),
            dma((2,)),
            dma((n_grp - 1,)), dma((n_grp - 1,)),
            dma, dma,
            dma((n_grp - 1,)), dma((n_grp - 1,)),
            dma((2, half_z, 2)), dma((2, half_z, 2)),
            dma((n_z + 1, 2)), dma((n_z + 1, 2)),
            dma((n_x - 1,)), dma((n_x - 1,)),
            dma, dma,
            dma((NY - 1,)), dma((NY - 1,)),
            dma((2, half_x)), dma((2, half_x)),
            dma((n_x - 1,)), dma((n_x - 1,)),
            dma((NY - 1,)), dma((NY - 1,)),
        ],
        compiler_params=pltpu.CompilerParams(collective_id=0, has_side_effects=True),
        name="update",
    )(coords, coords, blocks, factor_b, factor_c)


def sweep_kernel(m_ref, a_ref, g_ref, out_ref):
    gram_b, gram_c = g_ref[0], g_ref[1]
    down = lax.broadcasted_iota(jnp.int32, (R, R), 0)
    across = lax.broadcasted_iota(jnp.int32, (R, R), 1)
    on_diag = down == across

    def diagonals(square):
        kept = jnp.where(on_diag, square, 0.0)
        return jnp.sum(kept, axis=0, keepdims=True), jnp.sum(kept, axis=1, keepdims=True)

    b_row, b_col = diagonals(gram_b)
    c_row, c_col = diagonals(gram_c)
    b_row, b_col = jnp.sqrt(b_row), jnp.sqrt(b_col)
    c_row, c_col = jnp.sqrt(c_row), jnp.sqrt(c_col)
    gram = gram_b / (b_col * b_row) * (gram_c / (c_col * c_row))
    target = m_ref[...] / (b_row * c_row)
    pivot_row, pivot_col = diagonals(gram)
    later = jnp.where(down > across, gram, 0.0)
    known = jnp.dot(
        a_ref[...], later, precision=lax.Precision.HIGHEST, preferred_element_type=jnp.float32
    )
    start = ((target - known) / pivot_row).T
    weight = jnp.where(down > across, gram / pivot_col, 0.0)
    tiles = [start[8 * k : 8 * k + 8, :] for k in range(R // 8)]
    weights = [weight[8 * k : 8 * k + 8, :] for k in range(R // 8)]
    for r in range(R):
        own, sub = r // 8, r % 8
        fixed = jnp.maximum(jnp.broadcast_to(tiles[own][sub : sub + 1, :], (8, BS)), 0.0)
        for k in range(own, R // 8):
            if k == own and sub == 7:
                continue
            scale = jnp.broadcast_to(weights[k][:, r : r + 1], (8, BS))
            tiles[k] = tiles[k] - scale * fixed
    out_ref[...] = jnp.maximum(jnp.concatenate(tiles, axis=0), 0.0).T


def sweep(mttkrp, factor_a, gram):
    vmem = pl.BlockSpec(memory_space=pltpu.VMEM)
    return pl.pallas_call(
        sweep_kernel,
        out_shape=jax.ShapeDtypeStruct((BS, R), jnp.float32),
        in_specs=[vmem] * 3,
        out_specs=vmem,
        name="sweep",
    )(mttkrp, factor_a, gram)


def body(blocks, coords, factor_a, factor_b, factor_c):
    n_x, n_z = lax.axis_size("grp") // NC, lax.axis_size("rep") // NY
    mttkrp, gram = update(coords, blocks, factor_b, factor_c, n_x, n_z)
    return sweep(mttkrp, factor_a, gram)


def solution(mesh):
    placed = (
        P(("grp", "rep"), None, None),
        P(("grp", "rep"), None),
        P(("grp", "rep"), None),
        P("grp", None),
        P("grp", None),
    )
    return jax.shard_map(
        body, mesh=mesh, in_specs=placed, out_specs=P(("grp", "rep"), None), check_vma=False
    )
```

time: 99 us -> 76.5 us (0.77)
  the two profiles are of different devices: /device:TPU:24 before, /device:TPU:8 now
where the time goes in v2:
time: 76.5 us; the launch traced here: 76.3 us
  Pallas kernels  76.3 us (100%)
    pallas_call x1, Pallas kernels, update(): pl.pallas_call(functools.partial(update_kernel, n_x, n_z), out_shape=(jax...  73 us
    pallas_call x1, Pallas kernels, sweep(): pl.pallas_call(sweep_kernel, out_shape=jax.ShapeDtypeStruct((BS, R), jnp....  3.29 us

profile of v2, /device:TPU:8, one launch (start us, length us, event | category | flops | bytes accessed | tf_op | source)
XLA Modules:
  0.0 76.3 jit_solution(15893385688515153927)
XLA Ops:
  0.0 73.0 %update.1 = (f32[64,128]{1,0:T(8,128)}, f32[2,128,128]{2,1,0:T(8,128)}) custom-call(s32[2,3]{1,0:T(2,128)} %coords_sm.1, s32[2,3]{1,0:T(2,128)} %coords_sm.1, bf16[2,64,4096]{2,1,0:T(8,128)(2,1)} %blocks_ref.1, bf16[16,64,128]{2,1,0:T(8,128)(2,1)} %bitcast.2, bf16[16,64,128]{2,1,0:T(8,128)(2,1)} %bitcast.3), custom_call_target="tpu_custom_call" | custom-call | tf_op jit(solution)/shard_map/update/pallas_call | solution.py:343
  73.0 3.3 %sweep.1 = f32[64,128]{1,0:T(8,128)} custom-call(f32[64,128]{1,0:T(8,128)} %get-tuple-element.7.m_ref, f32[64,128]{1,0:T(8,128)} %a_ref.1, f32[2,128,128]{2,1,0:T(8,128)} %get-tuple-element.8.g_ref), custom_call_target="tpu_custom_call" | custom-call | tf_op jit(solution)/shard_map/sweep/pallas_call | solution.py:426

commit v3 on v2

--- a/solution.py
+++ b/solution.py
@@ -11,7 +11,7 @@
 BS = 64
 NC = 2
 NY = 8
-ROWS_Y = 24
+ROWS_Z = 32
 MESH = pl.DeviceIdType.MESH
 
 
@@ -64,24 +64,21 @@
 
 def update_kernel(
     n_x, n_z, coords_ref, coords_sm, blocks_ref, b_ref, c_ref, out_ref, gsum_ref,
-    cbuf, blocks, table, picked, rows_in, khatri, load, held, dense,
-    gpart, gbuf, gfin, land_y, land_x, land_x2, land_y2, part_y, part_x,
-    local, ks, kr, ts, tr, fs, fr, zs, zr, cs, cr, gs, gr, hs, hr,
-    ys, yr, xs, xr, x2s, x2r, y2s, y2r,
+    cbuf, blocks, table, picked, rows_in, khatri, load_z, load_y, held_z, held_y, dense_z, dense_y,
+    sums_z, sums_y, plan_z, plan_y, sm_z, sm_y,
+    gpart, gbuf, gfin, land_xz, land_xy, land_z, land_y,
+    local, ks, kr, ts, tr, fs, fr, zs, zr, cs, cr, vs, vr, ds, dr, gs, gr, hs, hr,
+    xzs, xzr, xys, xyr, zzs, zzr, yys, yyr,
 ):
     grp, rep = lax.axis_index("grp"), lax.axis_index("rep")
     n_grp = n_x * NC
     my_x, my_c = grp // NC, lax.rem(grp, NC)
     my_z, my_y = rep // NY, lax.rem(rep, NY)
-    half_z = n_z // 2
     jblocks = b_ref.shape[0]
     chip_blocks = NC * jblocks
 
-    def z_at(offset):
-        return lax.rem(my_z + (offset + 2 * n_z), n_z)
-
-    def z_peer(offset):
-        return {"grp": grp, "rep": z_at(offset) * NY + my_y}
+    def z_peer(z):
+        return {"grp": grp, "rep": z * NY + my_y}
 
     def y_peer(y):
         return {"grp": grp, "rep": my_z * NY + y}
@@ -108,9 +105,11 @@
     barrier = pltpu.get_barrier_semaphore()
     greeted = [grp_peer(lax.rem(grp + k, n_grp)) for k in range(1, n_grp)]
     greeted += [y_peer(lax.rem(my_y + k, NY)) for k in range(1, NY)]
-    greeted += [z_peer(k) for k in (1, -1, 2, -2)]
+    greeted += [z_peer(lax.rem(my_z + k, n_z)) for k in range(1, n_z)]
     for who in greeted:
         pl.semaphore_signal(barrier, inc=1, device_id=who, device_id_type=MESH)
+    for blank in (sums_z, sums_y, plan_z, plan_y):
+        blank[...] = jnp.zeros_like(blank)
     pl.semaphore_wait(barrier, len(greeted))
 
     sent = []
@@ -175,46 +174,52 @@
     for copy in answered:
         copy.wait_recv()
 
-    z_live, c_live = {}, {}
-
-    def carried(distance, way, piece):
-        return distance < half_z or piece == way
-
-    def pass_on(distance, way, piece):
-        sign = 1 if way == 0 else -1
-        hop = min(distance, 2)
-        origin = z_at(-sign * (distance - hop))
-        src = load.at[piece] if distance <= 2 else held.at[origin, my_c, piece]
-        z_live[distance, way, piece] = remote(
-            src, held.at[origin, my_c, piece],
-            zs.at[way, distance - 1, piece], zr.at[way, distance - 1, piece],
-            z_peer(sign * hop),
-        )
-
-    def hand_over(offset, piece):
-        origin = z_at(offset)
-        src = load.at[piece] if offset == 0 else held.at[origin, my_c, piece]
-        slot = offset + half_z
-        c_live[offset, piece] = remote(
-            src, held.at[origin, my_c, piece], cs.at[slot, piece], cr.at[slot, piece], partner
-        )
-
     for piece in range(2):
         left = rows_in[lax.div(coords_sm[piece, 1], chip_blocks), 0, piece].astype(jnp.float32)
         right = rows_in[lax.div(coords_sm[piece, 2], chip_blocks), 1, piece].astype(jnp.float32)
         for j in range(BS):
             khatri[j * BS : (j + 1) * BS, :] = (left[j : j + 1, :] * right).astype(jnp.bfloat16)
         partial = jnp.dot(blocks[piece], khatri[...], preferred_element_type=jnp.float32)
-        mark = jnp.full((8, R), coords_sm[piece, 0], jnp.int32).astype(jnp.float32)
-        load[piece, 0:BS, :] = partial
-        load[piece, BS : BS + 8, :] = mark
-        for distance in (2, 1):
-            for way in range(2):
-                if distance <= half_z and carried(distance, way, piece):
-                    pass_on(distance, way, piece)
-        hand_over(0, piece)
-        held[my_z, my_c, piece, 0:BS, :] = partial
-        held[my_z, my_c, piece, BS : BS + 8, :] = mark
+        mark = jnp.full((4, R), coords_sm[piece, 0], jnp.int32).astype(jnp.float32)
+        for load, low, high in ((load_z, 0, ROWS_Z), (load_y, ROWS_Z, BS)):
+            count = high - low
+            load[piece * count : (piece + 1) * count, :] = partial[low:high, :]
+            load[2 * count + 4 * piece : 2 * count + 4 * piece + 4, :] = mark
+
+    def far_first(n):
+        return sorted(range(1, n), key=lambda k: -min(k, n - k))
+
+    def arm(load, held, n, me, peer, send, recv, csend, crecv):
+        live, handed = {}, {}
+
+        def give(k):
+            live[k] = remote(
+                load, held.at[me, my_c], send.at[k - 1], recv.at[k - 1], peer(lax.rem(me + k, n))
+            )
+
+        def hand(k):
+            origin = lax.rem(me + (n - k), n)
+            src = load if k == 0 else held.at[origin, my_c]
+            handed[k] = remote(src, held.at[origin, my_c], csend.at[k], crecv.at[k], partner)
+
+        return live, handed, give, hand
+
+    live_z, handed_z, give_z, hand_z = arm(
+        load_z, held_z, n_z, my_z, z_peer, zs, zr, cs, cr
+    )
+    live_y, handed_y, give_y, hand_y = arm(
+        load_y, held_y, NY, my_y, y_peer, vs, vr, ds, dr
+    )
+    order_z, order_y = far_first(n_z), far_first(NY)
+    for index in range(max(n_z, NY) - 1):
+        if index < n_z - 1:
+            give_z(order_z[index])
+        if index < NY - 1:
+            give_y(order_y[index])
+    hand_y(0)
+    hand_z(0)
+    held_z[my_z, my_c] = load_z[...]
+    held_y[my_y, my_c] = load_y[...]
 
     gram_live = [
         remote(
@@ -224,119 +229,133 @@
     ]
     gbuf[my_x] = gpart[...]
 
-    def absorb(offset, first):
-        origin = z_at(offset)
-        marks = [held[origin, c, b, BS : BS + 8, :] for c in range(NC) for b in range(2)]
-        for part in range(2):
-            rows = slice(part * (BS // 2), (part + 1) * (BS // 2))
-            parts = [held[origin, c, b, rows, :] for c in range(NC) for b in range(2)]
-
-            def place(slot, carry):
-                x, y = slot // NY, lax.rem(slot, NY)
-                target = ((x * NC + my_c) * (n_z * NY) + my_z * NY + y).astype(jnp.float32)
-                total = None if first else dense[x, y, rows, :]
-                for mark, block in zip(marks, parts):
-                    hit = jnp.concatenate([mark == target] * (BS // 16), axis=0)
-                    term = jnp.where(hit, block, 0.0)
-                    total = term if total is None else total + term
-                dense[x, y, rows, :] = total
-                return carry
-
-            lax.fori_loop(0, n_x * NY, place, 0)
-
-    waiting = [0]
-    fresh = True
-    for distance in range(1, half_z + 1):
-        arrived = []
-        for offset in waiting:
-            for piece in range(2):
-                c_live[offset, piece].wait_recv()
-            absorb(offset, fresh)
-            fresh = False
-        for piece in range(2):
-            for way in range(2):
-                if not carried(distance, way, piece):
-                    continue
-                z_live[distance, way, piece].wait_recv()
-                onward = distance + 2
-                if onward <= half_z and carried(onward, way, piece):
-                    pass_on(onward, way, piece)
-                offset = -distance if way == 0 or distance == half_z else distance
-                hand_over(offset, piece)
-                if offset not in arrived:
-                    arrived.append(offset)
-        waiting = arrived
-    for offset in waiting:
-        for piece in range(2):
-            c_live[offset, piece].wait_recv()
-        absorb(offset, fresh)
+    def target_z(x, y):
+        return (x * NC + my_c) * (n_z * NY) + my_z * NY + y
+
+    def target_y(x, z):
+        return (x * NC + my_c) * (n_z * NY) + z * NY + my_y
+
+    def settle(held, sums, dense, plan, plan_sm, sem, n, count, target_of):
+        n_slot, n_load = dense.shape[1], n * NC * 2
+        lane = lax.broadcasted_iota(jnp.int32, (1, R), 1)
+        marks = [
+            held[o, c, 2 * count + 4 * b : 2 * count + 4 * b + 1, :]
+            for o in range(n) for c in range(NC) for b in range(2)
+        ]
+        x = sum((lane >= i * n_slot).astype(jnp.int32) for i in range(1, n_x))
+        target = target_of(x, lane - x * n_slot).astype(jnp.float32)
+        held_by = jnp.zeros((1, R), jnp.float32)
+        for k in range(n_load):
+            held_by = jnp.where(lane == k, marks[k], held_by)
+        first = jnp.full((1, R), n_load, jnp.int32)
+        following = jnp.full((1, R), n_load, jnp.int32)
+        for k in reversed(range(n_load)):
+            first = jnp.where(marks[k] == target, k, first)
+            same = jnp.logical_and(marks[k] == held_by, lane < k)
+            following = jnp.where(same, k, following)
+        plan[0:1, :] = first
+        plan[1:2, :] = following
+        copy = pltpu.make_async_copy(plan, plan_sm, sem)
+        copy.start()
+        copy.wait()
+
+        def chain(step, carry):
+            o = n - 1 - step
+            for c in reversed(range(NC)):
+                for b in reversed(range(2)):
+                    k = (o * NC + c) * 2 + b
+                    block = held[o, c, b * count : (b + 1) * count, :]
+                    sums[k] = block + sums[plan_sm[1, k]]
+            return carry
+
+        lax.fori_loop(0, n, chain, 0)
+
+        def place(other, carry):
+            for x in range(n_x):
+                dense[x, other] = sums[plan_sm[0, x * n_slot + other]]
+            return carry
+
+        lax.fori_loop(0, n_slot, place, 0)
+
+    def collect(live, handed, hand, order, between):
+        for index, k in enumerate(order):
+            live[k].wait_recv()
+            hand(k)
+            if index == len(order) // 2:
+                between()
+        for copy in handed.values():
+            copy.wait_recv()
+
+    def ring(dense, land, send, recv):
+        return Ring(
+            n_x, my_x, x_peer,
+            lambda x, low, high: dense.at[x, :, low:high, :],
+            lambda way, step, low, high: land.at[way, step, :, low:high, :],
+            send, recv, (0, dense.shape[2]),
+        )
 
     def spread(n, me, peer, source, land, send, recv):
-        order = sorted(range(1, n), key=lambda k: -min(k, n - k))
         live = []
-        for k in order:
+        for k in far_first(n):
             to = lax.rem(me + k, n)
-            live.append(remote(source(to), land.at[k - 1], send.at[k - 1], recv.at[k - 1], peer(to)))
+            live.append(
+                remote(source.at[my_x, to], land.at[k - 1], send.at[k - 1], recv.at[k - 1], peer(to))
+            )
         return live
 
-    y_first = spread(
-        NY, my_y, y_peer, lambda y: dense.at[:, y, 0:ROWS_Y, :], land_y, ys, yr
-    )
-    x_first = Ring(
-        n_x, my_x, x_peer,
-        lambda x, low, high: dense.at[x, :, low:high, :],
-        lambda way, step, low, high: land_x.at[way, step, :, low - ROWS_Y : high - ROWS_Y, :],
-        xs, xr, (ROWS_Y, BS),
-    )
-    x_first.start(1)
+    ring_y = ring(dense_y, land_xy, xys, xyr)
+    ring_z = ring(dense_z, land_xz, xzs, xzr)
+    collect(live_y, handed_y, hand_y, order_y, lambda: None)
+    settle(held_y, sums_y, dense_y, plan_y, sm_y, local.at[2], NY, BS - ROWS_Z, target_y)
+    ring_y.start(1)
     for copy in gram_live:
         copy.wait_recv()
     gram = gbuf[0]
     for x in range(1, n_x):
         gram = gram + gbuf[x]
     gsum_ref[my_c] = gram
-    gpart_all = gfin.at[0]
-    gpart_all[...] = gram
-    gram_over = remote(gpart_all, gfin.at[1], hs, hr, partner)
-    for step in range(1, x_first.half):
-        x_first.finish(step)
-        x_first.start(step + 1)
-    x_first.finish(x_first.half)
-    part_x[...] = dense[my_x, :, ROWS_Y:BS, :]
-    y_last = spread(NY, my_y, y_peer, lambda y: part_x.at[y], land_y2, y2s, y2r)
-    for copy in y_first:
-        copy.wait_recv()
-    for x in range(n_x):
-        total = dense[x, my_y, 0:ROWS_Y, :]
-        for k in range(NY - 1):
-            total = total + land_y[k, x]
-        part_y[x] = total
-    x_last = spread(n_x, my_x, x_peer, lambda x: part_y.at[x], land_x2, x2s, x2r)
+    gfin[0] = gram
+    gram_over = remote(gfin.at[0], gfin.at[1], hs, hr, partner)
+
+    def turn_y():
+        for step in range(1, n_x // 2):
+            ring_y.finish(step)
+            ring_y.start(step + 1)
+
+    collect(live_z, handed_z, hand_z, order_z, turn_y)
+    settle(held_z, sums_z, dense_z, plan_z, sm_z, local.at[3], n_z, ROWS_Z, target_z)
+    ring_z.start(1)
+    for step in range(1, n_x // 2):
+        ring_z.finish(step)
+        ring_z.start(step + 1)
+    ring_y.finish(n_x // 2)
+    last_y = spread(n_z, my_z, z_peer, dense_y, land_y, yys, yyr)
+    ring_z.finish(n_x // 2)
+    last_z = spread(NY, my_y, y_peer, dense_z, land_z, zzs, zzr)
     gram_over.wait_recv()
     gsum_ref[1 - my_c] = gfin[1]
-    for copy in x_last:
-        copy.wait_recv()
-    total = part_y[my_x]
-    for k in range(n_x - 1):
-        total = total + land_x2[k]
-    out_ref[0:ROWS_Y, :] = total
-    for copy in y_last:
-        copy.wait_recv()
-    total = part_x[my_y]
-    for k in range(NY - 1):
-        total = total + land_y2[k]
-    out_ref[ROWS_Y:BS, :] = total
+    for live, land, own, low, high in (
+        (last_z, land_z, dense_z.at[my_x, my_y], 0, ROWS_Z),
+        (last_y, land_y, dense_y.at[my_x, my_z], ROWS_Z, BS),
+    ):
+        for copy in live:
+            copy.wait_recv()
+        total = own[...]
+        for k in range(len(live)):
+            total = total + land[k]
+        out_ref[low:high, :] = total
     for copy in sent:
         copy.wait_send()
-    x_first.drain()
+    ring_y.drain()
+    ring_z.drain()
 
 
 def update(coords, blocks, factor_b, factor_c, n_x, n_z):
-    half_z, half_x, n_grp = n_z // 2, n_x // 2, n_x * NC
+    half_x, n_grp = n_x // 2, n_x * NC
     vmem = pl.BlockSpec(memory_space=pltpu.VMEM)
     anywhere = pl.BlockSpec(memory_space=pl.ANY)
     dma = pltpu.SemaphoreType.DMA
-    rest = BS - ROWS_Y
+    rest = BS - ROWS_Z
     f32, bf16 = jnp.float32, jnp.bfloat16
     factor_b, factor_c = factor_b.reshape(-1, BS, R), factor_c.reshape(-1, BS, R)
     jblocks = factor_b.shape[0]
@@ -355,30 +374,39 @@
             pltpu.VMEM((n_grp - 1, 2, BS, R), bf16),
             pltpu.VMEM((n_x, NC, 2, BS, R), bf16),
             pltpu.VMEM((BS * BS, R), bf16),
-            pltpu.VMEM((2, BS + 8, R), f32),
-            pltpu.VMEM((n_z, NC, 2, BS + 8, R), f32),
-            pltpu.VMEM((n_x, NY, BS, R), f32),
+            pltpu.VMEM((2 * ROWS_Z + 8, R), f32),
+            pltpu.VMEM((2 * rest + 8, R), f32),
+            pltpu.VMEM((n_z, NC, 2 * ROWS_Z + 8, R), f32),
+            pltpu.VMEM((NY, NC, 2 * rest + 8, R), f32),
+            pltpu.VMEM((n_x, NY, ROWS_Z, R), f32),
+            pltpu.VMEM((n_x, n_z, rest, R), f32),
+            pltpu.VMEM((n_z * NC * 2 + 1, ROWS_Z, R), f32),
+            pltpu.VMEM((NY * NC * 2 + 1, rest, R), f32),
+            pltpu.VMEM((8, R), jnp.int32),
+            pltpu.VMEM((8, R), jnp.int32),
+            pltpu.SMEM((8, R), jnp.int32),
+            pltpu.SMEM((8, R), jnp.int32),
             pltpu.VMEM((R, R), f32),
             pltpu.VMEM((n_x, R, R), f32),
             pltpu.VMEM((2, R, R), f32),
-            pltpu.VMEM((NY - 1, n_x, ROWS_Y, R), f32),
-            pltpu.VMEM((2, half_x, NY, rest, R), f32),
-            pltpu.VMEM((n_x - 1, ROWS_Y, R), f32),
-            pltpu.VMEM((NY - 1, rest, R), f32),
-            pltpu.VMEM((n_x, ROWS_Y, R), f32),
-            pltpu.VMEM((NY, rest, R), f32),
-            dma((2,)),
+            pltpu.VMEM((2, half_x, NY, ROWS_Z, R), f32),
+            pltpu.VMEM((2, half_x, n_z, rest, R), f32),
+            pltpu.VMEM((NY - 1, ROWS_Z, R), f32),
+            pltpu.VMEM((n_z - 1, rest, R), f32),
+            dma((4,)),
             dma((n_grp - 1,)), dma((n_grp - 1,)),
             dma, dma,
             dma((n_grp - 1,)), dma((n_grp - 1,)),
-            dma((2, half_z, 2)), dma((2, half_z, 2)),
-            dma((n_z + 1, 2)), dma((n_z + 1, 2)),
+            dma((n_z - 1,)), dma((n_z - 1,)),
+            dma((n_z,)), dma((n_z,)),
+            dma((NY - 1,)), dma((NY - 1,)),
+            dma((NY,)), dma((NY,)),
             dma((n_x - 1,)), dma((n_x - 1,)),
             dma, dma,
+            dma((2, half_x)), dma((2, half_x)),
+            dma((2, half_x)), dma((2, half_x)),
             dma((NY - 1,)), dma((NY - 1,)),
-            dma((2, half_x)), dma((2, half_x)),
-            dma((n_x - 1,)), dma((n_x - 1,)),
-            dma((NY - 1,)), dma((NY - 1,)),
+            dma((n_z - 1,)), dma((n_z - 1,)),
         ],
         compiler_params=pltpu.CompilerParams(collective_id=0, has_side_effects=True),
         name="update",

time: 76.5 us -> 65.7 us (0.86)
  the two profiles are of different devices: /device:TPU:8 before, /device:TPU:1 now
where the time goes in v3:
time: 65.7 us; the launch traced here: 65.6 us
  Pallas kernels  65.6 us (100%)
    pallas_call x1, Pallas kernels, update(): pl.pallas_call(functools.partial(update_kernel, n_x, n_z), out_shape=(jax...  62.3 us
    pallas_call x1, Pallas kernels, sweep(): pl.pallas_call(sweep_kernel, out_shape=jax.ShapeDtypeStruct((BS, R), jnp....  3.29 us

profile of v3, /device:TPU:1, one launch (start us, length us, event | category | flops | bytes accessed | tf_op | source)
XLA Modules:
  0.0 65.6 jit_solution(2047234378906689332)
XLA Ops:
  0.0 62.3 %update.1 = (f32[64,128]{1,0:T(8,128)}, f32[2,128,128]{2,1,0:T(8,128)}) custom-call(s32[2,3]{1,0:T(2,128)} %coords_sm.1, s32[2,3]{1,0:T(2,128)} %coords_sm.1, bf16[2,64,4096]{2,1,0:T(8,128)(2,1)} %blocks_ref.1, bf16[16,64,128]{2,1,0:T(8,128)(2,1)} %bitcast.2, bf16[16,64,128]{2,1,0:T(8,128)(2,1)} %bitcast.3), custom_call_target="tpu_custom_call" | custom-call | tf_op jit(solution)/shard_map/update/pallas_call | solution.py:362
  62.3 3.3 %sweep.1 = f32[64,128]{1,0:T(8,128)} custom-call(f32[64,128]{1,0:T(8,128)} %get-tuple-element.7.m_ref, f32[64,128]{1,0:T(8,128)} %a_ref.1, f32[2,128,128]{2,1,0:T(8,128)} %get-tuple-element.8.g_ref), custom_call_target="tpu_custom_call" | custom-call | tf_op jit(solution)/shard_map/sweep/pallas_call | solution.py:454

commit v4 on v3

--- a/solution.py
+++ b/solution.py
@@ -62,11 +62,34 @@
             copy.wait_send()
 
 
+def prepare(gram_b, gram_c, a_ref, known, rows, weight_ref):
+    down = lax.broadcasted_iota(jnp.int32, (R, R), 0)
+    across = lax.broadcasted_iota(jnp.int32, (R, R), 1)
+
+    def diagonals(square):
+        kept = jnp.where(down == across, square, 0.0)
+        return jnp.sum(kept, axis=0, keepdims=True), jnp.sum(kept, axis=1, keepdims=True)
+
+    b_row, b_col = diagonals(gram_b)
+    c_row, c_col = diagonals(gram_c)
+    b_row, b_col = jnp.sqrt(b_row), jnp.sqrt(b_col)
+    c_row, c_col = jnp.sqrt(c_row), jnp.sqrt(c_col)
+    gram = gram_b / (b_col * b_row) * (gram_c / (c_col * c_row))
+    pivot_row, pivot_col = diagonals(gram)
+    later = jnp.where(down > across, gram, 0.0)
+    known[...] = jnp.dot(
+        a_ref[...], later, precision=lax.Precision.HIGHEST, preferred_element_type=jnp.float32
+    )
+    rows[0:1, :] = b_row * c_row
+    rows[1:2, :] = pivot_row
+    weight_ref[...] = jnp.where(down > across, gram / pivot_col, 0.0)
+
+
 def update_kernel(
-    n_x, n_z, coords_ref, coords_sm, blocks_ref, b_ref, c_ref, out_ref, gsum_ref,
-    cbuf, blocks, table, picked, rows_in, khatri, load_z, load_y, held_z, held_y, dense_z, dense_y,
+    n_x, n_z, coords_hbm, blocks_ref, b_ref, c_ref, a_hbm, out_ref, weight_ref,
+    coords_ref, coords_sm, a_ref, cbuf, blocks, table, picked, rows_in, khatri, load_z, load_y, held_z, held_y, dense_z, dense_y,
     sums_z, sums_y, plan_z, plan_y, sm_z, sm_y,
-    gpart, gbuf, gfin, land_xz, land_xy, land_z, land_y,
+    gpart, gbuf, gfin, gsum, known, rows, land_xz, land_xy, land_z, land_y,
     local, ks, kr, ts, tr, fs, fr, zs, zr, cs, cr, vs, vr, ds, dr, gs, gr, hs, hr,
     xzs, xzr, xys, xyr, zzs, zzr, yys, yyr,
 ):
@@ -92,15 +115,18 @@
     partner = grp_peer(my_x * NC + (1 - my_c))
     own_rows = pl.ds(my_c * jblocks, jblocks)
     fetch_blocks = pltpu.make_async_copy(blocks_ref, blocks, local.at[0])
-    fetch_blocks.start()
-
-    @pl.when(my_c == 0)
-    def _():
-        pltpu.make_async_copy(b_ref, table.at[own_rows], local.at[1]).start()
-
-    @pl.when(my_c != 0)
-    def _():
-        pltpu.make_async_copy(c_ref, table.at[own_rows], local.at[1]).start()
+    fetch_coords = pltpu.make_async_copy(coords_hbm, coords_ref, local.at[4])
+    fetch_own = pltpu.make_async_copy(coords_hbm, coords_sm, local.at[5])
+    fetch_a = pltpu.make_async_copy(a_hbm, a_ref, local.at[6])
+
+    def own_part():
+        @pl.when(my_c == 0)
+        def _():
+            pltpu.make_async_copy(b_ref, table.at[own_rows], local.at[1]).start()
+
+        @pl.when(my_c != 0)
+        def _():
+            pltpu.make_async_copy(c_ref, table.at[own_rows], local.at[1]).start()
 
     barrier = pltpu.get_barrier_semaphore()
     greeted = [grp_peer(lax.rem(grp + k, n_grp)) for k in range(1, n_grp)]
@@ -108,8 +134,13 @@
     greeted += [z_peer(lax.rem(my_z + k, n_z)) for k in range(1, n_z)]
     for who in greeted:
         pl.semaphore_signal(barrier, inc=1, device_id=who, device_id_type=MESH)
+    for copy in (fetch_coords, fetch_own, fetch_blocks, fetch_a):
+        copy.start()
+    own_part()
     for blank in (sums_z, sums_y, plan_z, plan_y):
         blank[...] = jnp.zeros_like(blank)
+    fetch_coords.wait()
+    fetch_own.wait()
     pl.semaphore_wait(barrier, len(greeted))
 
     sent = []
@@ -123,13 +154,17 @@
         sent.append(copy)
         return copy
 
-    asked = [
-        remote(
+    def far_first(n):
+        return sorted(range(1, n), key=lambda k: -min(k, n - k))
+
+    order_g = far_first(n_grp)
+    asked = {
+        k: remote(
             coords_ref, cbuf.at[grp], ks.at[k - 1], kr.at[k - 1],
             grp_peer(lax.rem(grp + k, n_grp)),
         )
-        for k in range(1, n_grp)
-    ]
+        for k in order_g
+    }
 
     def share(ref):
         return pltpu.make_async_remote_copy(
@@ -153,8 +188,8 @@
         return table[lax.rem(q, chip_blocks)]
 
     answered = []
-    for k in range(1, n_grp):
-        asked[k - 1].wait_recv()
+    for k in order_g:
+        asked[k].wait_recv()
         asker = lax.rem(grp + (n_grp - k), n_grp)
         for b in range(2):
             picked[k - 1, b] = look_up(cbuf[asker, b, 1 + my_c])
@@ -167,9 +202,6 @@
     for b in range(2):
         rows_in[my_x, my_c, b] = look_up(coords_sm[b, 1 + my_c])
 
-    dims = (((0,), (0,)), ((), ()))
-    whole = table[...].reshape(chip_blocks * BS, R)
-    gpart[...] = lax.dot_general(whole, whole, dims, preferred_element_type=jnp.float32)
     fetch_blocks.wait()
     for copy in answered:
         copy.wait_recv()
@@ -185,9 +217,6 @@
             count = high - low
             load[piece * count : (piece + 1) * count, :] = partial[low:high, :]
             load[2 * count + 4 * piece : 2 * count + 4 * piece + 4, :] = mark
-
-    def far_first(n):
-        return sorted(range(1, n), key=lambda k: -min(k, n - k))
 
     def arm(load, held, n, me, peer, send, recv, csend, crecv):
         live, handed = {}, {}
@@ -221,6 +250,9 @@
     held_z[my_z, my_c] = load_z[...]
     held_y[my_y, my_c] = load_y[...]
 
+    dims = (((0,), (0,)), ((), ()))
+    whole = table[...].reshape(chip_blocks * BS, R)
+    gpart[...] = lax.dot_general(whole, whole, dims, preferred_element_type=jnp.float32)
     gram_live = [
         remote(
             gpart, gbuf.at[my_x], gs.at[k - 1], gr.at[k - 1], x_peer(lax.rem(my_x + k, n_x))
@@ -313,7 +345,7 @@
     gram = gbuf[0]
     for x in range(1, n_x):
         gram = gram + gbuf[x]
-    gsum_ref[my_c] = gram
+    gsum[my_c] = gram
     gfin[0] = gram
     gram_over = remote(gfin.at[0], gfin.at[1], hs, hr, partner)
 
@@ -321,36 +353,38 @@
         for step in range(1, n_x // 2):
             ring_y.finish(step)
             ring_y.start(step + 1)
+        gram_over.wait_recv()
+        gsum[1 - my_c] = gfin[1]
+        fetch_a.wait()
+        prepare(gsum[0], gsum[1], a_ref, known, rows, weight_ref)
 
     collect(live_z, handed_z, hand_z, order_z, turn_y)
     settle(held_z, sums_z, dense_z, plan_z, sm_z, local.at[3], n_z, ROWS_Z, target_z)
     ring_z.start(1)
+    ring_y.finish(n_x // 2)
+    last_y = spread(n_z, my_z, z_peer, dense_y, land_y, yys, yyr)
     for step in range(1, n_x // 2):
         ring_z.finish(step)
         ring_z.start(step + 1)
-    ring_y.finish(n_x // 2)
-    last_y = spread(n_z, my_z, z_peer, dense_y, land_y, yys, yyr)
     ring_z.finish(n_x // 2)
     last_z = spread(NY, my_y, y_peer, dense_z, land_z, zzs, zzr)
-    gram_over.wait_recv()
-    gsum_ref[1 - my_c] = gfin[1]
     for live, land, own, low, high in (
+        (last_y, land_y, dense_y.at[my_x, my_z], ROWS_Z, BS),
         (last_z, land_z, dense_z.at[my_x, my_y], 0, ROWS_Z),
-        (last_y, land_y, dense_y.at[my_x, my_z], ROWS_Z, BS),
     ):
         for copy in live:
             copy.wait_recv()
         total = own[...]
         for k in range(len(live)):
             total = total + land[k]
-        out_ref[low:high, :] = total
+        out_ref[low:high, :] = (total / rows[0:1, :] - known[low:high, :]) / rows[1:2, :]
     for copy in sent:
         copy.wait_send()
     ring_y.drain()
     ring_z.drain()
 
 
-def update(coords, blocks, factor_b, factor_c, n_x, n_z):
+def update(coords, blocks, factor_b, factor_c, factor_a, n_x, n_z):
     half_x, n_grp = n_x // 2, n_x * NC
     vmem = pl.BlockSpec(memory_space=pltpu.VMEM)
     anywhere = pl.BlockSpec(memory_space=pl.ANY)
@@ -363,11 +397,14 @@
         functools.partial(update_kernel, n_x, n_z),
         out_shape=(
             jax.ShapeDtypeStruct((BS, R), f32),
-            jax.ShapeDtypeStruct((2, R, R), f32),
+            jax.ShapeDtypeStruct((R, R), f32),
         ),
-        in_specs=[vmem, pl.BlockSpec(memory_space=pltpu.SMEM), anywhere, anywhere, anywhere],
+        in_specs=[anywhere] * 5,
         out_specs=(vmem, vmem),
         scratch_shapes=[
+            pltpu.VMEM(coords.shape, jnp.int32),
+            pltpu.SMEM(coords.shape, jnp.int32),
+            pltpu.VMEM((BS, R), f32),
             pltpu.SMEM((n_grp,) + coords.shape, jnp.int32),
             pltpu.VMEM(blocks.shape, bf16),
             pltpu.VMEM((NC * jblocks, BS, R), bf16),
@@ -389,11 +426,14 @@
             pltpu.VMEM((R, R), f32),
             pltpu.VMEM((n_x, R, R), f32),
             pltpu.VMEM((2, R, R), f32),
+            pltpu.VMEM((2, R, R), f32),
+            pltpu.VMEM((BS, R), f32),
+            pltpu.VMEM((8, R), f32),
             pltpu.VMEM((2, half_x, NY, ROWS_Z, R), f32),
             pltpu.VMEM((2, half_x, n_z, rest, R), f32),
             pltpu.VMEM((NY - 1, ROWS_Z, R), f32),
             pltpu.VMEM((n_z - 1, rest, R), f32),
-            dma((4,)),
+            dma((7,)),
             dma((n_grp - 1,)), dma((n_grp - 1,)),
             dma, dma,
             dma((n_grp - 1,)), dma((n_grp - 1,)),
@@ -410,32 +450,11 @@
         ],
         compiler_params=pltpu.CompilerParams(collective_id=0, has_side_effects=True),
         name="update",
-    )(coords, coords, blocks, factor_b, factor_c)
-
-
-def sweep_kernel(m_ref, a_ref, g_ref, out_ref):
-    gram_b, gram_c = g_ref[0], g_ref[1]
-    down = lax.broadcasted_iota(jnp.int32, (R, R), 0)
-    across = lax.broadcasted_iota(jnp.int32, (R, R), 1)
-    on_diag = down == across
-
-    def diagonals(square):
-        kept = jnp.where(on_diag, square, 0.0)
-        return jnp.sum(kept, axis=0, keepdims=True), jnp.sum(kept, axis=1, keepdims=True)
-
-    b_row, b_col = diagonals(gram_b)
-    c_row, c_col = diagonals(gram_c)
-    b_row, b_col = jnp.sqrt(b_row), jnp.sqrt(b_col)
-    c_row, c_col = jnp.sqrt(c_row), jnp.sqrt(c_col)
-    gram = gram_b / (b_col * b_row) * (gram_c / (c_col * c_row))
-    target = m_ref[...] / (b_row * c_row)
-    pivot_row, pivot_col = diagonals(gram)
-    later = jnp.where(down > across, gram, 0.0)
-    known = jnp.dot(
-        a_ref[...], later, precision=lax.Precision.HIGHEST, preferred_element_type=jnp.float32
-    )
-    start = ((target - known) / pivot_row).T
-    weight = jnp.where(down > across, gram / pivot_col, 0.0)
+    )(coords, blocks, factor_b, factor_c, factor_a)
+
+
+def sweep_kernel(start_ref, weight_ref, out_ref):
+    start, weight = start_ref[...].T, weight_ref[...]
     tiles = [start[8 * k : 8 * k + 8, :] for k in range(R // 8)]
     weights = [weight[8 * k : 8 * k + 8, :] for k in range(R // 8)]
     for r in range(R):
@@ -449,21 +468,21 @@
     out_ref[...] = jnp.maximum(jnp.concatenate(tiles, axis=0), 0.0).T
 
 
-def sweep(mttkrp, factor_a, gram):
+def sweep(start, weight):
     vmem = pl.BlockSpec(memory_space=pltpu.VMEM)
     return pl.pallas_call(
         sweep_kernel,
         out_shape=jax.ShapeDtypeStruct((BS, R), jnp.float32),
-        in_specs=[vmem] * 3,
+        in_specs=[vmem] * 2,
         out_specs=vmem,
         name="sweep",
-    )(mttkrp, factor_a, gram)
+    )(start, weight)
 
 
 def body(blocks, coords, factor_a, factor_b, factor_c):
     n_x, n_z = lax.axis_size("grp") // NC, lax.axis_size("rep") // NY
-    mttkrp, gram = update(coords, blocks, factor_b, factor_c, n_x, n_z)
-    return sweep(mttkrp, factor_a, gram)
+    start, weight = update(coords, blocks, factor_b, factor_c, factor_a, n_x, n_z)
+    return sweep(start, weight)
 
 
 def solution(mesh):

time: 65.7 us -> 65.3 us (level)
  no operation moved by 1% of the time
where the time goes in v4:
time: 65.3 us; the launch traced here: 65.1 us
  Pallas kernels  65.1 us (100%)
    pallas_call x1, Pallas kernels, update(): pl.pallas_call(functools.partial(update_kernel, n_x, n_z), out_shape=(jax...  62.1 us
    pallas_call x1, Pallas kernels, sweep(): pl.pallas_call(sweep_kernel, out_shape=jax.ShapeDtypeStruct((BS, R), jnp....  2.99 us

profile of v4, /device:TPU:1, one launch (start us, length us, event | category | flops | bytes accessed | tf_op | source)
XLA Modules:
  0.0 65.1 jit_solution(3110089982974580954)
XLA Ops:
  0.0 62.1 %update.1 = (f32[64,128]{1,0:T(8,128)}, f32[128,128]{1,0:T(8,128)}) custom-call(s32[2,3]{1,0:T(2,128)} %coords_hbm.1, bf16[2,64,4096]{2,1,0:T(8,128)(2,1)} %blocks_ref.1, bf16[16,64,128]{2,1,0:T(8,128)(2,1)} %bitcast.2, bf16[16,64,128]{2,1,0:T(8,128)(2,1)} %bitcast.3, f32[64,128]{1,0:T(8,128)} %a_hbm.1), custom_call_target="tpu_custom_call" | custom-call | tf_op jit(solution)/shard_map/update/pallas_call | solution.py:396
  62.1 3.0 %sweep.1 = f32[64,128]{1,0:T(8,128)} custom-call(f32[64,128]{1,0:T(8,128)} %get-tuple-element.7.start_ref, f32[128,128]{1,0:T(8,128)} %get-tuple-element.8.weight_ref), custom_call_target="tpu_custom_call" | custom-call | tf_op jit(solution)/shard_map/sweep/pallas_call | solution.py:473

commit v5 on v4

--- a/solution.py
+++ b/solution.py
@@ -302,12 +302,17 @@
 
         lax.fori_loop(0, n, chain, 0)
 
-        def place(other, carry):
-            for x in range(n_x):
-                dense[x, other] = sums[plan_sm[0, x * n_slot + other]]
-            return carry
-
-        lax.fori_loop(0, n_slot, place, 0)
+        def place(steps):
+            def slot(other, carry):
+                for step in steps:
+                    x = lax.rem(my_x + step, n_x)
+                    dense[x, other] = sums[plan_sm[0, x * n_slot + other]]
+                return carry
+
+            lax.fori_loop(0, n_slot, slot, 0)
+
+        place([n_x // 2])
+        return lambda: place([step for step in range(n_x) if step != n_x // 2])
 
     def collect(live, handed, hand, order, between):
         for index, k in enumerate(order):
@@ -338,8 +343,9 @@
     ring_y = ring(dense_y, land_xy, xys, xyr)
     ring_z = ring(dense_z, land_xz, xzs, xzr)
     collect(live_y, handed_y, hand_y, order_y, lambda: None)
-    settle(held_y, sums_y, dense_y, plan_y, sm_y, local.at[2], NY, BS - ROWS_Z, target_y)
+    rest_y = settle(held_y, sums_y, dense_y, plan_y, sm_y, local.at[2], NY, BS - ROWS_Z, target_y)
     ring_y.start(1)
+    rest_y()
     for copy in gram_live:
         copy.wait_recv()
     gram = gbuf[0]
@@ -353,16 +359,17 @@
         for step in range(1, n_x // 2):
             ring_y.finish(step)
             ring_y.start(step + 1)
-        gram_over.wait_recv()
-        gsum[1 - my_c] = gfin[1]
-        fetch_a.wait()
-        prepare(gsum[0], gsum[1], a_ref, known, rows, weight_ref)
 
     collect(live_z, handed_z, hand_z, order_z, turn_y)
-    settle(held_z, sums_z, dense_z, plan_z, sm_z, local.at[3], n_z, ROWS_Z, target_z)
+    rest_z = settle(held_z, sums_z, dense_z, plan_z, sm_z, local.at[3], n_z, ROWS_Z, target_z)
     ring_z.start(1)
+    rest_z()
     ring_y.finish(n_x // 2)
     last_y = spread(n_z, my_z, z_peer, dense_y, land_y, yys, yyr)
+    gram_over.wait_recv()
+    gsum[1 - my_c] = gfin[1]
+    fetch_a.wait()
+    prepare(gsum[0], gsum[1], a_ref, known, rows, weight_ref)
     for step in range(1, n_x // 2):
         ring_z.finish(step)
         ring_z.start(step + 1)

time: 65.3 us -> 65.5 us (level)
  no operation moved by 1% of the time
where the time goes in v5:
time: 65.5 us; the launch traced here: 65.3 us
  Pallas kernels  65.3 us (100%)
    pallas_call x1, Pallas kernels, update(): pl.pallas_call(functools.partial(update_kernel, n_x, n_z), out_shape=(jax...  62.3 us
    pallas_call x1, Pallas kernels, sweep(): pl.pallas_call(sweep_kernel, out_shape=jax.ShapeDtypeStruct((BS, R), jnp....  2.99 us

profile of v5, /device:TPU:1, one launch (start us, length us, event | category | flops | bytes accessed | tf_op | source)
XLA Modules:
  0.0 65.3 jit_solution(839325042818815530)
XLA Ops:
  0.0 62.3 %update.1 = (f32[64,128]{1,0:T(8,128)}, f32[128,128]{1,0:T(8,128)}) custom-call(s32[2,3]{1,0:T(2,128)} %coords_hbm.1, bf16[2,64,4096]{2,1,0:T(8,128)(2,1)} %blocks_ref.1, bf16[16,64,128]{2,1,0:T(8,128)(2,1)} %bitcast.2, bf16[16,64,128]{2,1,0:T(8,128)(2,1)} %bitcast.3, f32[64,128]{1,0:T(8,128)} %a_hbm.1), custom_call_target="tpu_custom_call" | custom-call | tf_op jit(solution)/shard_map/update/pallas_call | solution.py:403
  62.3 3.0 %sweep.1 = f32[64,128]{1,0:T(8,128)} custom-call(f32[64,128]{1,0:T(8,128)} %get-tuple-element.7.start_ref, f32[128,128]{1,0:T(8,128)} %get-tuple-element.8.weight_ref), custom_call_target="tpu_custom_call" | custom-call | tf_op jit(solution)/shard_map/sweep/pallas_call | solution.py:480
